TPU v7x, 256 devices: a whole 4x4x8 slice. The times are simulated.
256 devices in a mesh: seq: 64 (over y, z, x_hi), mp: 4 (over x_lo, core).
Axes of the slice: x: 4 (x_hi: 2, x_lo: 2; x = x_hi * 2 + x_lo), y: 4, z: 8, core: 2. Of those that a mesh axis runs over, the one named last changes fastest.
Arguments:
- stream: bfloat16 [20480, 1024], P('seq'), as said below
- gain_attn: float32 [1024], replicated, may hold values from 0.1 to 1.9
- gain_mlp: float32 [1024], replicated, may hold values from 0.1 to 1.9
- gain_read: float32 [1024], replicated, may hold values from 0.1 to 1.9
- query_weight: bfloat16 [1024, 1024], P(None, 'mp'), as said below
- key_weight: bfloat16 [1024, 1024], P(None, 'mp'), as said below
- value_weight: bfloat16 [1024, 1024], P(None, 'mp'), may hold values from -0.1875 to 0.1875
- out_weight: bfloat16 [1024, 1024], P('mp'), may hold values from -0.1875 to 0.1875
- up_weight: bfloat16 [1024, 2048], P(None, 'mp'), may hold values from -0.1875 to 0.1875
- down_weight: bfloat16 [2048, 1024], P('mp'), may hold values from -0.125 to 0.125
- read_weight: bfloat16 [1024, 8192], P(None, 'mp'), may hold values from -0.1875 to 0.1875
- read_bias: float32 [8192], P('mp'), may hold values from -3 to 3
- spike_counts: int32 [20480, 8192], P('seq', 'mp'), may hold values from 0 to 7
Outputs:
- log_rate: bfloat16 [20480, 8192], P('seq', 'mp')
- poisson_loss: float32 [20480], P('seq')
Inputs may be any that keep to these rules, and one draw needn't show every extreme that they name: Real-valued residual stream. `query_weight`: Real-valued projection. `key_weight`: Real-valued projection.
All inputs are finite; a program needn't handle non-finite values.
Results may differ from a plain program's by a relative error of at most 0.014.
Values may be sent and summed in bfloat16 or wider, within the bound.
A program may use at most 128 MiB of HBM per device.

v0:
```python
import jax
import jax.numpy as jnp
from jax import lax
from jax.sharding import PartitionSpec as P

DH = 64
NEU = 8192


def rms_norm(field, gain):
    wide = field.astype(jnp.float32)
    scale = lax.rsqrt(jnp.mean(wide * wide, axis=-1, keepdims=True) + 1e-05)
    return wide * scale * gain


def per_device(
    stream,
    gain_attn,
    gain_mlp,
    gain_read,
    query_weight,
    key_weight,
    value_weight,
    out_weight,
    up_weight,
    down_weight,
    read_weight,
    read_bias,
    spike_counts,
):
    shard_rows = stream.shape[0]
    my_index = lax.axis_index("seq")

    def position(device, within):
        return device * shard_rows + within

    normed = rms_norm(stream, gain_attn).astype(jnp.bfloat16)
    queries_flat = jnp.dot(normed, query_weight, preferred_element_type=jnp.float32).astype(
        jnp.bfloat16
    )
    keys_flat = jnp.dot(normed, key_weight, preferred_element_type=jnp.float32).astype(jnp.bfloat16)
    values_flat = jnp.dot(normed, value_weight, preferred_element_type=jnp.float32).astype(
        jnp.bfloat16
    )
    local_heads = queries_flat.shape[1] // DH
    factor = DH ** (-0.5)
    queries = queries_flat.reshape(shard_rows, local_heads, DH)
    query_pos = position(my_index, jnp.arange(shard_rows, dtype=jnp.int32))
    query_last = jnp.max(query_pos)
    init = (
        jnp.full((local_heads, shard_rows), -1e30, jnp.float32),
        jnp.zeros((local_heads, shard_rows), jnp.float32),
        jnp.zeros((local_heads, shard_rows, DH), jnp.float32),
    )
    state = init
    keys_piece = lax.all_gather(keys_flat, "seq", axis=0, tiled=True)
    values_piece = lax.all_gather(values_flat, "seq", axis=0, tiled=True)
    piece_rows = keys_piece.shape[0]
    gathered_rows = jnp.arange(piece_rows, dtype=jnp.int32)
    key_pos = position(gathered_rows // shard_rows, gathered_rows % shard_rows)
    block_rows = 512
    block_count = piece_rows // block_rows

    def one_block(inner_state, block_index):
        offset = block_index * block_rows
        key_block = lax.dynamic_slice_in_dim(keys_piece, offset, block_rows, 0).reshape(
            block_rows, local_heads, DH
        )
        value_block = lax.dynamic_slice_in_dim(values_piece, offset, block_rows, 0).reshape(
            block_rows, local_heads, DH
        )
        block_pos = lax.dynamic_slice_in_dim(key_pos, offset, block_rows, 0)

        def update(current):
            best, total_weight, accum = current
            scores = (
                jnp.einsum("qhd,khd->hqk", queries, key_block, preferred_element_type=jnp.float32)
                * factor
            )
            allowed = block_pos[None, None, :] <= query_pos[None, :, None]
            scores = jnp.where(allowed, scores, -1e30)
            fresh = jnp.maximum(best, jnp.max(scores, axis=-1))
            weights = jnp.where(allowed, jnp.exp(scores - fresh[..., None]), 0.0)
            decay = jnp.exp(best - fresh)
            total_weight = total_weight * decay + jnp.sum(weights, axis=-1)
            weights_low = weights.astype(jnp.bfloat16)
            accum = accum * decay[..., None] + jnp.einsum(
                "hqk,khd->hqd", weights_low, value_block, preferred_element_type=jnp.float32
            )
            return (fresh, total_weight, accum)

        def keep(current):
            return current

        return (lax.cond(jnp.min(block_pos) > query_last, keep, update, inner_state), None)

    state, unused = lax.scan(one_block, state, jnp.arange(block_count, dtype=jnp.int32))
    best, total_weight, accum = state
    attended = (
        jnp.transpose(accum / total_weight[..., None], (1, 0, 2))
        .reshape(shard_rows, local_heads * DH)
        .astype(jnp.bfloat16)
    )
    attn_part = jnp.dot(attended, out_weight, preferred_element_type=jnp.float32)
    attn_total = lax.psum(attn_part.astype(jnp.bfloat16), "mp").astype(jnp.float32)
    resid = (stream.astype(jnp.float32) + attn_total).astype(jnp.bfloat16)
    mlp_in = rms_norm(resid, gain_mlp).astype(jnp.bfloat16)
    hidden = jax.nn.gelu(
        jnp.dot(mlp_in, up_weight, preferred_element_type=jnp.float32), approximate=True
    ).astype(jnp.bfloat16)
    mlp_part = jnp.dot(hidden, down_weight, preferred_element_type=jnp.float32)
    outcome = resid.astype(jnp.float32) + lax.psum(mlp_part.astype(jnp.bfloat16), "mp").astype(
        jnp.float32
    )
    read_in = rms_norm(outcome, gain_read).astype(jnp.bfloat16)
    rate_full = jnp.dot(read_in, read_weight, preferred_element_type=jnp.float32) + read_bias
    loss_part = jnp.sum(jnp.exp(rate_full) - spike_counts.astype(jnp.float32) * rate_full, axis=-1)
    poisson_loss = lax.psum(loss_part, "mp") / NEU
    return (rate_full.astype(jnp.bfloat16), poisson_loss)


def solution(mesh):
    in_specs = (
        P("seq", None),
        P(),
        P(),
        P(),
        P(None, "mp"),
        P(None, "mp"),
        P(None, "mp"),
        P("mp", None),
        P(None, "mp"),
        P("mp", None),
        P(None, "mp"),
        P("mp"),
        P("seq", "mp"),
    )
    out_specs = (P("seq", "mp"), P("seq"))
    return jax.shard_map(
        per_device, mesh=mesh, in_specs=in_specs, out_specs=out_specs, check_vma=False
    )
```

profile of v0, /device:TPU:1, one launch (start us, length us, event | category | flops | bytes accessed | tf_op | source)
XLA Modules:
  0.0 773.9 jit_solution(6381487957085612974)
XLA Ops:
  7.3 1.5 fusion.14
  8.7 2.3 convolution_convert_fusion.4
  11.2 1.1 convolution_convert_fusion.2
  13.6 165.9 %all-gather.3.cloned.1.call-done = bf16[20480,256]{1,0:T(8,128)(2,1)} async-done(((bf16[320,256]{1,0:T(8,128)(2,1)}), bf16[20480,256]{1,0:T(8,128)(2,1)}) %all-gather.3.cloned.1.call-update) | async-done | bytes 10485776 | tf_op jit(solution)/shard_map/all_gather | solution.py:56
  179.5 14.2 %copy.19 = bf16[20480,256]{0,1:T(8,128)(2,1)} copy(bf16[20480,256]{1,0:T(8,128)(2,1)} %all-gather.3.cloned.1.call-done) | data formatting | bytes 20971520
  193.7 150.1 %all-gather.5.cloned.1.call-done = bf16[20480,256]{1,0:T(8,128)(2,1)} async-done(((bf16[320,256]{1,0:T(8,128)(2,1)}), bf16[20480,256]{1,0:T(8,128)(2,1)}) %all-gather.5.cloned.1.call-update) | async-done | bytes 10485776 | tf_op jit(solution)/shard_map/all_gather | solution.py:57
  343.8 14.2 %copy.20 = bf16[20480,256]{0,1:T(8,128)(2,1)} copy(bf16[20480,256]{1,0:T(8,128)(2,1)} %all-gather.5.cloned.1.call-done) | data formatting | bytes 20971520
  358.1 138.6 %while.15 = (s32[]{:T(128)}, f32[4,320]{1,0:T(4,128)S(1)}, f32[4,320]{1,0:T(4,128)S(1)}, f32[4,320,64]{1,2,0:T(8,128)S(1)}, s32[40]{0:T(128)S(1)}, /*index=5*/s3...) while((s32[]{:T(128)}, f32[4,320]{1,0:T(4,128)S(1)}, ...), condition=%wide.region_8.9_spmd.clone, body=%wide.region_2.8_spmd.clone.sunk | while | flops 176622912 | bytes 11005285 | solution.py:97
  359.4 0.7 fusion.75
  361.4 4.3 conditional.3
  361.6 1.3 constant_dynamic-slice_fusion
  363.0 0.7 fusion.2
  363.7 1.0 fusion.4
  364.7 1.0 fusion.8
  367.0 0.7 fusion.75
  370.4 0.7 fusion.75
  373.7 0.7 fusion.75
  377.1 0.7 fusion.75
  380.4 0.7 fusion.75
  383.8 0.7 fusion.75
  387.2 0.7 fusion.75
  390.5 0.7 fusion.75
  393.9 0.7 fusion.75
  397.2 0.7 fusion.75
  496.8 1.2 convolution_convert_fusion.1
  498.0 206.9 %all-reduce.3.cloned.1.call-done = bf16[320,1024]{1,0:T(8,128)(2,1)} async-done(((bf16[320,1024]{1,0:T(8,128)(2,1)}), bf16[320,1024]{1,0:T(8,128)(2,1)}) %all-reduce.3.cloned.1.call-update) | async-done | bytes 655376 | tf_op jit(solution)/shard_map/psum | solution.py:105
  705.0 1.4 fusion.18
  706.4 3.1 convolution_convert_fusion
  709.6 44.4 %all-reduce.5.cloned.1.call-done = bf16[320,1024]{1,0:T(8,128)(2,1)} async-done(((bf16[320,1024]{1,0:T(8,128)(2,1)}), bf16[320,1024]{1,0:T(8,128)(2,1)}) %all-reduce.5.cloned.1.call-update) | async-done | bytes 655376 | tf_op jit(solution)/shard_map/psum | solution.py:112
  754.0 1.4 multiply_reduce_fusion
  755.4 6.2 subtract_reduce_fusion
  761.6 5.1 psum.23
  (270 shorter events, 48.9 us)
Async XLA Ops:
  7.2 699.2 %copy-start = (bf16[512,1024]{1,0:T(8,128)(2,1)S(1)}, bf16[512,1024]{1,0:T(8,128)(2,1)}, u32[]{:S(2)}) copy-start(bf16[512,1024]{1,0:T(8,128)(2,1)} %param.26) | copy-start | bytes 3145732
  7.2 4.0 copy-start.1
  7.2 4.0 copy-start.6
  7.2 4.0 copy-start.3
  7.2 5.1 copy-start.4
  7.2 172.3 %all-gather.3.cloned.1.call-start = ((), (), s32[]{:S(2)}) async-start(), calls=%async_computation | async-start | bytes 10649600 | tf_op jit(solution)/shard_map/all_gather | solution.py:56
  11.1 332.7 %all-gather.5.cloned.1.call-start = ((), (), s32[]{:S(2)}) async-start(), calls=%async_computation.1 | async-start | bytes 10649600 | tf_op jit(solution)/shard_map/all_gather | solution.py:57
  12.2 692.7 %all-reduce.3.cloned.1.call-start = ((), (), s32[]{:S(2)}) async-start(), calls=%async_computation.2 | async-start | bytes 1310720 | tf_op jit(solution)/shard_map/psum | solution.py:105
  358.1 138.7 %copy-start.2 = (bf16[256,1024]{1,0:T(8,128)(2,1)S(1)}, bf16[256,1024]{1,0:T(8,128)(2,1)}, u32[]{:S(2)}) copy-start(bf16[256,1024]{1,0:T(8,128)(2,1)} %param.24) | copy-start | bytes 1572868
  496.7 209.7 %copy-start.7 = (f32[1024]{0:T(1024)S(1)}, f32[1024]{0:T(1024)}, u32[]{:S(2)}) copy-start(f32[1024]{0:T(1024)} %param.19) | copy-start | bytes 12292
  498.0 256.0 %all-reduce.5.cloned.1.call-start = ((), (), s32[]{:S(2)}) async-start(), calls=%async_computation.3 | async-start | bytes 1310720 | tf_op jit(solution)/shard_map/psum | solution.py:112
  706.4 49.0 %copy-start.5 = (f32[2048]{0:T(1024)S(1)}, f32[2048]{0:T(1024)}, u32[]{:S(2)}) copy-start(f32[2048]{0:T(1024)} %param.28) | copy-start | bytes 24580
  706.4 49.0 %copy-start.8 = (f32[1024]{0:T(1024)S(1)}, f32[1024]{0:T(1024)}, u32[]{:S(2)}) copy-start(f32[1024]{0:T(1024)} %param.20) | copy-start | bytes 12292
Sparse Core Ops, SparseCore 0:
  12.1 167.3 all-gather.2
  183.0 160.7 all-gather.4
  498.1 206.7 all-reduce.2
  709.7 44.2 all-reduce.4
where the time goes:
time: 777 us; the launch traced here: 774 us
  waiting for transfers between devices  567 us (73%)
  loops' own time  81 us (10%)
  local copies, waits for them, and re-layouts  53.8 us (7%)
  other arithmetic  36.5 us (5%)
  matrix products  16 us (2%)
  between operations  14 us (2%)
    psum x1, waiting for transfers between devices, per_device(): lax.psum(attn_part.astype(jnp.bfloat16), 'mp').astype(jnp.float32)  207 us
    all_gather x1, waiting for transfers between devices, per_device(): keys_piece = lax.all_gather(keys_flat, 'seq', axis=0, tiled=True)  166 us
    all_gather x1, waiting for transfers between devices, per_device(): values_piece = lax.all_gather(values_flat, 'seq', axis=0, tiled=True)  150 us
    another operation x1, loops' own time, per_device(): lax.scan(one_block, state, jnp.arange(block_count, dtype=jnp.int32))  79.8 us
    psum x1, waiting for transfers between devices, per_device(): lax.psum(mlp_part.astype(jnp.bfloat16), 'mp').astype(jnp.float32)  44.4 us
    reduce_min x40, other arithmetic, one_block(): jnp.min(block_pos) > query_last  29.6 us
    unnamed x20, local copies, waits for them, and re-layouts  28.5 us
    dynamic_slice x40, local copies, waits for them, and re-layouts, per_device(): lax.scan(one_block, state, jnp.arange(block_count, dtype=jnp.int32))  23.5 us
  transfers between devices with their start and end apart: 4, of which 4 were waited for; matrix products, arithmetic and copies ran while one was open for 2% of the time, Pallas kernels for 0%

commit v1 on v0

--- a/solution.py
+++ b/solution.py
@@ -5,6 +5,13 @@
 
 DH = 64
 NEU = 8192
+
+
+def gather_over(shard, name, d):
+    size = lax.axis_size(name)
+    blocks = jnp.stack([shard for _ in range(size)])
+    blocks = lax.all_to_all(blocks, name, split_axis=0, concat_axis=0)
+    return jnp.concatenate(blocks, axis=d)
 
 
 def rms_norm(field, gain):
@@ -54,7 +61,7 @@
     )
     state = init
     keys_piece = lax.all_gather(keys_flat, "seq", axis=0, tiled=True)
-    values_piece = lax.all_gather(values_flat, "seq", axis=0, tiled=True)
+    values_piece = gather_over(values_flat, "seq", 0)
     piece_rows = keys_piece.shape[0]
     gathered_rows = jnp.arange(piece_rows, dtype=jnp.int32)
     key_pos = position(gathered_rows // shard_rows, gathered_rows % shard_rows)

time: 777 us -> 751 us (0.967)
  waiting for transfers between devices: 567 us -> 524 us
  starting transfers between devices: 0.16 us -> 15.6 us
    all_to_all x0 -> x1, waiting for transfers between devices: none -> 271 us  [gather_over(): blocks = lax.all_to_all(blocks, name, split_axis=0, concat_axis=0)]
    all_gather x1, waiting for transfers between devices: 166 us -> 0.01 us  [per_device(): keys_piece = lax.all_gather(keys_flat, 'seq', axis=0, tiled=True)]
    all_gather x1 -> x0, waiting for transfers between devices: 150 us -> none  [per_device(): values_piece = lax.all_gather(values_flat, 'seq', axis=0, tiled=True)]
    all_to_all x0 -> x1, starting transfers between devices: none -> 15.5 us  [gather_over(): blocks = lax.all_to_all(blocks, name, split_axis=0, concat_axis=0)]
  transfers between devices with their start and end apart: 4 -> 4, of which waited for: 4 -> 3; matrix products, arithmetic and copies ran while one was open for 2% -> 2% of each run, Pallas kernels for 0% -> 0%
where the time goes in v1:
time: 751 us; the launch traced here: 748 us
  waiting for transfers between devices  524 us (70%)
  loops' own time  78.7 us (10%)
  local copies, waits for them, and re-layouts  59.1 us (8%)
  other arithmetic  36.4 us (5%)
  starting transfers between devices  15.6 us (2%)
  matrix products  15.3 us (2%)
  between operations  13.9 us (2%)
    all_to_all x1, waiting for transfers between devices, gather_over(): blocks = lax.all_to_all(blocks, name, split_axis=0, concat_axis=0)  271 us
    psum x1, waiting for transfers between devices, per_device(): lax.psum(attn_part.astype(jnp.bfloat16), 'mp').astype(jnp.float32)  209 us
    another operation x1, loops' own time, per_device(): lax.scan(one_block, state, jnp.arange(block_count, dtype=jnp.int32))  77.6 us
    psum x1, waiting for transfers between devices, per_device(): lax.psum(mlp_part.astype(jnp.bfloat16), 'mp').astype(jnp.float32)  44.4 us
    reduce_min x40, other arithmetic, one_block(): jnp.min(block_pos) > query_last  29.6 us
    unnamed x20, local copies, waits for them, and re-layouts  28.6 us
    dynamic_slice x40, local copies, waits for them, and re-layouts, per_device(): lax.scan(one_block, state, jnp.arange(block_count, dtype=jnp.int32))  23.5 us
    all_to_all x1, starting transfers between devices, gather_over(): blocks = lax.all_to_all(blocks, name, split_axis=0, concat_axis=0)  15.5 us
  transfers between devices with their start and end apart: 4, of which 3 were waited for; matrix products, arithmetic and copies ran while one was open for 2% of the time, Pallas kernels for 0%

profile of v1, /device:TPU:1, one launch (start us, length us, event | category | flops | bytes accessed | tf_op | source)
XLA Modules:
  0.0 748.0 jit_solution(16132447292197089451)
XLA Ops:
  7.2 1.4 fusion.14
  8.6 1.6 convolution_convert_fusion.2
  10.2 5.3 stack.2
  15.5 15.5 %all-to-all-start = ((bf16[64,320,256]{2,1,0:T(8,128)(2,1)}), bf16[64,320,256]{2,1,0:T(8,128)(2,1)}, u32[]{:S(2)}, u32[]{:S(2)}) async-start(bf16[64,320,256]{2,1,0:T(8,128)(2,1)} %stack.2), calls=%async_computation | async-start | bytes 20971520 | tf_op jit(solution)/shard_map/all_to_all | solution.py:13
  31.1 1.1 convolution_convert_fusion.4
  33.5 270.6 %all-to-all-done = bf16[64,320,256]{2,1,0:T(8,128)(2,1)} async-done(((bf16[64,320,256]{2,1,0:T(8,128)(2,1)}), bf16[64,320,256]{2,1,0:T(8,128)(2,1)}, u32[]{:S(2)}, u32[]{:S(2)}) %all-to-all-start) | async-done | bytes 10485792 | tf_op jit(solution)/shard_map/all_to_all | solution.py:13
  304.1 14.3 %copy.20 = bf16[20480,256]{0,1:T(8,128)(2,1)} copy(bf16[20480,256]{1,0:T(8,128)(2,1)} %bitcast.4) | data formatting | bytes 20971520
  318.4 14.2 %copy.19 = bf16[20480,256]{0,1:T(8,128)(2,1)} copy(bf16[20480,256]{1,0:T(8,128)(2,1)} %all-gather.2.cloned.1.call-done) | data formatting | bytes 20971520
  332.7 136.3 %while.15 = (s32[]{:T(128)}, f32[4,320]{1,0:T(4,128)S(1)}, f32[4,320]{1,0:T(4,128)S(1)}, f32[4,320,64]{1,2,0:T(8,128)S(1)}, s32[40]{0:T(128)S(1)}, /*index=5*/s3...) while((s32[]{:T(128)}, f32[4,320]{1,0:T(4,128)S(1)}, ...), condition=%wide.region_8.9_spmd.clone, body=%wide.region_2.8_spmd.clone.sunk | while | flops 176622912 | bytes 11005285 | solution.py:104
  334.0 0.7 fusion.75
  336.0 4.3 conditional.3
  336.2 1.3 constant_dynamic-slice_fusion
  337.5 0.7 fusion.2
  338.3 1.0 fusion.4
  339.3 1.0 fusion.8
  341.6 0.7 fusion.75
  344.9 0.7 fusion.75
  348.2 0.7 fusion.75
  351.5 0.7 fusion.75
  354.8 0.7 fusion.75
  358.1 0.7 fusion.75
  361.4 0.7 fusion.75
  364.7 0.7 fusion.75
  368.0 0.7 fusion.75
  469.1 1.2 convolution_convert_fusion.1
  470.4 208.7 %all-reduce.3.cloned.1.call-done = bf16[320,1024]{1,0:T(8,128)(2,1)} async-done(((bf16[320,1024]{1,0:T(8,128)(2,1)}), bf16[320,1024]{1,0:T(8,128)(2,1)}) %all-reduce.3.cloned.1.call-update) | async-done | bytes 655376 | tf_op jit(solution)/shard_map/psum | solution.py:112
  679.1 1.4 fusion.18
  680.5 3.1 convolution_convert_fusion
  683.7 44.4 %all-reduce.5.cloned.1.call-done = bf16[320,1024]{1,0:T(8,128)(2,1)} async-done(((bf16[320,1024]{1,0:T(8,128)(2,1)}), bf16[320,1024]{1,0:T(8,128)(2,1)}) %all-reduce.5.cloned.1.call-update) | async-done | bytes 655376 | tf_op jit(solution)/shard_map/psum | solution.py:119
  728.1 1.4 multiply_reduce_fusion
  729.5 6.2 subtract_reduce_fusion
  735.7 5.2 psum.23
  (270 shorter events, 49.5 us)
Async XLA Ops:
  7.2 673.3 %copy-start = (bf16[512,1024]{1,0:T(8,128)(2,1)S(1)}, bf16[512,1024]{1,0:T(8,128)(2,1)}, u32[]{:S(2)}) copy-start(bf16[512,1024]{1,0:T(8,128)(2,1)} %param.26) | copy-start | bytes 3145732
  15.5 15.6 %copy-start.1 = (bf16[320,1024]{1,0:T(8,128)(2,1)S(1)}, bf16[320,1024]{1,0:T(8,128)(2,1)}, u32[]{:S(2)}) copy-start(bf16[320,1024]{1,0:T(8,128)(2,1)} %param.17) | copy-start | bytes 1966084
  15.5 15.6 %copy-start.3 = (bf16[1024,256]{1,0:T(8,128)(2,1)S(1)}, bf16[1024,256]{1,0:T(8,128)(2,1)}, u32[]{:S(2)}) copy-start(bf16[1024,256]{1,0:T(8,128)(2,1)} %param.22) | copy-start | bytes 1572868
  15.5 15.6 %copy-start.6 = (f32[1024]{0:T(1024)S(1)}, f32[1024]{0:T(1024)}, u32[]{:S(2)}) copy-start(f32[1024]{0:T(1024)} %param.18) | copy-start | bytes 12292
  15.5 16.7 %copy-start.4 = (bf16[1024,256]{1,0:T(8,128)(2,1)S(1)}, bf16[1024,256]{1,0:T(8,128)(2,1)}, u32[]{:S(2)}) copy-start(bf16[1024,256]{1,0:T(8,128)(2,1)} %param.21) | copy-start | bytes 1572868
  15.5 288.6 %all-to-all-start = ((bf16[64,320,256]{2,1,0:T(8,128)(2,1)}), bf16[64,320,256]{2,1,0:T(8,128)(2,1)}, u32[]{:S(2)}, u32[]{:S(2)}) async-start(bf16[64,320,256]{2,1,0:T(8,128)(2,1)} %stack.2), calls=%async_computation | async-start | bytes 20971520 | tf_op jit(solution)/shard_map/all_to_all | solution.py:13
  31.0 287.4 %all-gather.2.cloned.1.call-start = ((), (), s32[]{:S(2)}) async-start(), calls=%async_computation.1 | async-start | bytes 10649600 | tf_op jit(solution)/shard_map/all_gather | solution.py:63
  32.2 646.9 %all-reduce.3.cloned.1.call-start = ((), (), s32[]{:S(2)}) async-start(), calls=%async_computation.2 | async-start | bytes 1310720 | tf_op jit(solution)/shard_map/psum | solution.py:112
  332.7 136.4 %copy-start.2 = (bf16[256,1024]{1,0:T(8,128)(2,1)S(1)}, bf16[256,1024]{1,0:T(8,128)(2,1)}, u32[]{:S(2)}) copy-start(bf16[256,1024]{1,0:T(8,128)(2,1)} %param.24) | copy-start | bytes 1572868
  469.0 211.5 %copy-start.7 = (f32[1024]{0:T(1024)S(1)}, f32[1024]{0:T(1024)}, u32[]{:S(2)}) copy-start(f32[1024]{0:T(1024)} %param.19) | copy-start | bytes 12292
  470.3 257.8 %all-reduce.5.cloned.1.call-start = ((), (), s32[]{:S(2)}) async-start(), calls=%async_computation.3 | async-start | bytes 1310720 | tf_op jit(solution)/shard_map/psum | solution.py:119
  680.5 49.0 %copy-start.5 = (f32[2048]{0:T(1024)S(1)}, f32[2048]{0:T(1024)}, u32[]{:S(2)}) copy-start(f32[2048]{0:T(1024)} %param.28) | copy-start | bytes 24580
  680.5 49.0 %copy-start.8 = (f32[1024]{0:T(1024)S(1)}, f32[1024]{0:T(1024)}, u32[]{:S(2)}) copy-start(f32[1024]{0:T(1024)} %param.20) | copy-start | bytes 12292
Sparse Core Ops, SparseCore 0:
  35.9 277.4 all-gather.1
  470.5 208.5 all-reduce.2
  683.8 44.2 all-reduce.4
